TPU v7x, 32 devices: a whole 2x2x4 slice. The times are simulated.
32 devices in a mesh: ctx: 8 (over y, x, core), exp: 4 (over z).
Axes of the slice: x: 2, y: 2, z: 4, core: 2. Of those that a mesh axis runs over, the one named last changes fastest.
Arguments:
- conv_input: bfloat16 [1024, 4096], P('ctx', 'exp'), may hold values from -6 to 6
- conv_weight: float32 [4, 4096], P(None, 'exp'), may hold values from -3 to 3
- b_proj: bfloat16 [1024, 128], P('ctx'), may hold values from -0.5 to 0.5
- c_proj: bfloat16 [1024, 128], P('ctx'), may hold values from -0.29882812 to 0.29882812
- log_decay: float32 [64, 1024], P('exp', 'ctx'), may hold values from -1 to 0
- skip_gain: float32 [64], P('exp'), may hold values from 0.5 to 1.5
- grad_in: bfloat16 [1024, 4096], P('ctx', 'exp'), may hold values from -6 to 6
- norm_gain: float32 [4096], replicated, may hold values from 0.1 to 1.9
- expert_ids: int32 [1024, 2], P('ctx'), may hold values from 0 to 3, all different within a row; in each aligned block of 32 rows (0 to 31, 32 to 63, ...) at most 24 rows name the same one
- expert_weights: float32 [1024, 2], P('ctx'), may hold values from 0.1 to 1
- up_weight: bfloat16 [4, 4096, 12288], P('exp', None, 'ctx'), may hold values from -0.09375 to 0.09375
- down_weight: bfloat16 [4, 12288, 4096], P('exp', 'ctx'), may hold values from -0.0546875 to 0.0546875
Outputs:
- moe_out: bfloat16 [1024, 4096], P('ctx', 'exp')
- grad_conv: float32 [1024, 4096], P('ctx', 'exp')
Inputs may be any that keep to these rules, and one draw needn't show every extreme that they name: `expert_ids`: each token names 2 different experts; in each aligned block of 32 tokens no expert is named more than 24 times.
All inputs are finite; a program needn't handle non-finite values.
Results may differ from a plain program's by a relative error of at most 0.018.
Values may be sent and summed in bfloat16 or wider, within the bound.
No kernel may reach another device: no remote copies, remote signals or barrier semaphores. Data moves between devices by JAX's collectives and lax.ppermute only.
A program may use at most 128 MiB of HBM per device.

v0:
```python
import jax
import jax.numpy as jnp
from jax import lax
from jax.sharding import PartitionSpec as P

CONV = 4
TOPK = 2
HIGHEST = lax.Precision.HIGHEST
EPSILON = 1e-06


def passed_along(block, axis, distance):
    devices = range(lax.axis_size(axis))
    route = [(i - distance, i) for i in devices if i - distance in devices]
    return lax.ppermute(block, axis, route)


def prefix(x, axis, combine, identity, reverse):
    size, mine = (lax.axis_size(axis), lax.axis_index(axis))
    everything = jax.tree.map(
        lambda part, kind: lax.all_gather(part.astype(kind), axis), x, (jnp.bfloat16, jnp.bfloat16)
    )
    start = jax.tree.map(
        lambda part, zero: jnp.broadcast_to(jnp.asarray(zero, part.dtype), part.shape), x, identity
    )

    def turn(k, before):
        at = size - 1 - k if reverse else k
        reached = at > mine if reverse else at < mine
        new = combine(
            before, jax.tree.map(lambda part, own: part[at].astype(own.dtype), everything, x)
        )
        return jax.tree.map(lambda a, b: jnp.where(reached, a, b), new, before)

    return lax.fori_loop(0, size, turn, start)


def combine_state(earlier, later):
    return (earlier[0] * later[0], later[0][:, None, None] * earlier[1] + later[1])


def conv_mix(extended, conv_weight):
    rows_out = extended.shape[0] - conv_weight.shape[0] + 1
    total = jnp.zeros((rows_out, extended.shape[1]), jnp.float32)
    for offset in range(conv_weight.shape[0]):
        total = total + conv_weight[offset][None, :] * extended[offset : offset + rows_out]
    return jax.nn.silu(total).astype(jnp.bfloat16)


def block_terms(decay_block, b_raw, c_raw):
    totals = jnp.cumsum(decay_block, axis=1)
    rows_here = totals.shape[1]
    causal = jnp.arange(rows_here)[:, None] >= jnp.arange(rows_here)[None, :]
    spread = jnp.where(causal[None], totals[:, :, None] - totals[:, None, :], 0.0)
    kernel = (
        jnp.where(causal[None], jnp.exp(spread), 0.0)
        * jnp.dot(c_raw, b_raw.T, preferred_element_type=jnp.float32)[None]
    )
    to_end = jnp.exp(totals[:, -1:] - totals)
    return (totals, kernel, to_end)


def normalize(rows_in, norm_gain):
    values = rows_in.astype(jnp.float32)
    scale = lax.rsqrt(jnp.mean(values * values, axis=1, keepdims=True) + EPSILON)
    return (values * scale * norm_gain[None, :]).astype(jnp.bfloat16)


def route_matrix(chosen_ids, slots_each, experts):
    pairs = chosen_ids.reshape(-1)
    onehot = (pairs[:, None] == jnp.arange(experts, dtype=jnp.int32)[None, :]).astype(jnp.int32)
    ranks = jnp.sum((jnp.cumsum(onehot, axis=0) - 1) * onehot, axis=1)
    target = pairs * slots_each + ranks
    return (jnp.arange(experts * slots_each, dtype=jnp.int32)[:, None] == target[None, :]).astype(
        jnp.bfloat16
    )


def gather_back(dispatch, returned, weights):
    values = jnp.einsum("sp,sc->pc", dispatch, returned, preferred_element_type=jnp.float32)
    values = values.reshape(weights.shape[0], weights.shape[1], returned.shape[1])
    return jnp.sum(weights[:, :, None] * values, axis=1).astype(jnp.bfloat16)


def expert_block(rows_in, up_weight, down_weight):
    up_local = up_weight[0]
    down_local = down_weight[0]
    hidden = jax.nn.silu(
        jnp.dot(
            lax.all_gather(rows_in, "ctx", axis=0, tiled=True),
            up_local,
            preferred_element_type=jnp.float32,
        )
    ).astype(jnp.bfloat16)
    summed = lax.psum_scatter(
        jnp.dot(hidden, down_local, preferred_element_type=jnp.float32).astype(jnp.bfloat16),
        "ctx",
        scatter_dimension=0,
        tiled=True,
    )
    return summed


def shards(
    conv_input,
    conv_weight,
    b_proj,
    c_proj,
    log_decay,
    skip_gain,
    grad_in,
    norm_gain,
    expert_ids,
    expert_weights,
    up_weight,
    down_weight,
):
    tok_rows = conv_input.shape[0]
    heads_here = log_decay.shape[0]
    head_size = conv_input.shape[1] // heads_here
    rim_rows = passed_along(conv_input[tok_rows - (CONV - 1) :], "ctx", 1)
    extended = jnp.concatenate(
        [rim_rows.astype(jnp.float32), conv_input.astype(jnp.float32)], axis=0
    )
    mixed_in = conv_mix(extended, conv_weight)
    inputs_block = mixed_in.astype(jnp.float32).reshape(tok_rows, heads_here, head_size)
    b_block = b_proj.astype(jnp.float32)
    c_block = c_proj.astype(jnp.float32)
    grad_block = grad_in.astype(jnp.float32).reshape(tok_rows, heads_here, head_size)
    totals, kernel, to_end = block_terms(log_decay, b_proj, c_proj)
    through = jnp.exp(totals[:, -1])
    local_state = jnp.einsum("hs,shp,sn->hpn", to_end, inputs_block, b_block, precision=HIGHEST)
    local_grad = jnp.einsum(
        "ht,thp,tn->hpn", jnp.exp(totals), grad_block, c_block, precision=HIGHEST
    )
    zero_state = jnp.zeros_like(local_state)
    ones_heads = jnp.ones_like(through)
    carry_state = prefix(
        (through, local_state), "ctx", combine_state, (ones_heads, zero_state), False
    )[1]
    carry_grad = prefix(
        (through, local_grad), "ctx", combine_state, (ones_heads, zero_state), True
    )[1]
    inner = jnp.einsum("hts,shp->thp", kernel, inputs_block, precision=HIGHEST)
    carried = jnp.exp(totals).T[:, :, None] * jnp.einsum(
        "hpn,tn->thp", carry_state, c_block, precision=HIGHEST
    )
    output = inner + carried + skip_gain[None, :, None] * inputs_block
    ssd_out = output.reshape(tok_rows, heads_here * head_size).astype(jnp.bfloat16)
    grad_inner = jnp.einsum("hts,thp->shp", kernel, grad_block, precision=HIGHEST)
    grad_carried = to_end.T[:, :, None] * jnp.einsum(
        "hpn,sn->shp", carry_grad, b_block, precision=HIGHEST
    )
    grad_conv = (grad_inner + grad_carried + skip_gain[None, :, None] * grad_block).reshape(
        tok_rows, heads_here * head_size
    )
    experts = lax.axis_size("exp")
    most_rows = 3 * TOPK * tok_rows // (2 * experts * experts)
    share = tok_rows // experts
    token_view = lax.all_to_all(ssd_out, "exp", split_axis=0, concat_axis=1, tiled=True)
    normed = normalize(token_view, norm_gain)
    first_row = lax.axis_index("exp") * share
    my_ids = lax.dynamic_slice_in_dim(expert_ids, first_row, share, 0)
    my_weights = lax.dynamic_slice_in_dim(expert_weights, first_row, share, 0)
    dispatch = route_matrix(my_ids, most_rows, experts)
    outgoing = jnp.dot(
        dispatch, jnp.repeat(normed, TOPK, axis=0), preferred_element_type=jnp.float32
    ).astype(jnp.bfloat16)
    incoming = lax.all_to_all(
        outgoing.reshape(experts, most_rows, normed.shape[1]),
        "exp",
        split_axis=0,
        concat_axis=0,
        tiled=True,
    )
    results = expert_block(
        incoming.reshape(experts * most_rows, normed.shape[1]), up_weight, down_weight
    )
    returned = lax.all_to_all(
        results.reshape(experts, most_rows, normed.shape[1]),
        "exp",
        split_axis=0,
        concat_axis=0,
        tiled=True,
    )
    combined = gather_back(
        dispatch, returned.reshape(experts * most_rows, normed.shape[1]), my_weights
    )
    moe_out = lax.all_to_all(combined, "exp", split_axis=1, concat_axis=0, tiled=True)
    return (moe_out, grad_conv)


def solution(mesh):
    placed = (
        P("ctx", "exp"),
        P(None, "exp"),
        P("ctx", None),
        P("ctx", None),
        P("exp", "ctx"),
        P("exp"),
        P("ctx", "exp"),
        P(),
        P("ctx", None),
        P("ctx", None),
        P("exp", None, "ctx"),
        P("exp", "ctx", None),
    )
    return jax.shard_map(
        shards,
        mesh=mesh,
        in_specs=placed,
        out_specs=(P("ctx", "exp"), P("ctx", "exp")),
        check_vma=False,
    )
```

profile of v0, /device:TPU:0, one launch (start us, length us, event | category | flops | bytes accessed | tf_op | source)
XLA Modules:
  0.0 299.9 jit_solution(15138509072731504501)
XLA Ops:
  7.2 0.7 slice.29
  8.0 2.3 collective-permute-start
  10.3 0.9 fusion.53
  11.2 1.0 reduce_window_sum.23
  12.5 1.0 convert_element_type.132
  13.5 0.3 multiply_convert_fusion.2
  14.0 1.9 convolution_convert_fusion.2
  15.9 1.2 dynamic-slice
  18.0 0.2 dynamic-update-slice
  18.3 14.5 %all-reduce = bf16[128]{0:T(256)(128)(2,1)S(1)} all-reduce(bf16[128]{0:T(256)(128)(2,1)S(1)} %dynamic-update-slice), channel_id=2, replica_groups=mesh['ctx'=8,'exp'=4] {'ctx'}, use_global_device_ids=true, to_apply=%add | all-reduce | flops 128 | bytes 512
  32.8 0.8 constant_dynamic-slice_fusion
  33.8 0.9 fusion.54
  34.8 11.8 %all-gather.9.cloned.1.call-done = bf16[128,64,128]{2,1,0:T(8,128)(2,1)} async-done(((bf16[16,64,128]{2,1,0:T(8,128)(2,1)}), bf16[128,64,128]{2,1,0:T(8,128)(2,1)}) %all-gather.9.cloned.1.call-update) | async-done | bytes 2097168 | tf_op jit(solution)/shard_map/all_gather | solution.py:21
  46.6 9.1 %while.30 = (s32[]{:T(128)}, f32[16,64,128]{2,1,0:T(8,128)S(1)}, s32[]{:T(128)}, bf16[8,16]{1,0:T(8,128)(2,1)S(1)}, bf16[8,16,64,128]{3,2,1,0:T(8,128)(2,1)}, /*index=5*/s32[]{:T(128)}, s32[]{:T(128)}) while((s32[]{:T(128)}, f32[16,64,128]{2,1,0:T(8,128)S(1)}, s32[]{:T(128)}, bf16[8,16]{1,0:T(8,128)(2,1)S(1)}, ...), condition=%wide.region_4.5_spmd.clone, body=%wide.region_3.4_spmd.clone.sunk | while | flops 655380 | bytes 1310985 | solution.py:35
  46.6 1.1 fusion.66
  47.7 1.1 fusion.66
  48.8 1.1 fusion.66
  50.0 1.1 fusion.66
  51.1 1.1 fusion.66
  52.3 1.1 fusion.66
  53.4 1.1 fusion.66
  54.5 1.1 fusion.66
  55.6 0.4 fusion.18
  56.0 1.3 fusion.20
  57.4 0.4 copy.35
  57.8 1.1 convert_element_type.138
  58.8 4.6 %all-to-all-start = ((bf16[4,32,1024]{2,1,0:T(8,128)(2,1)}), bf16[4,32,1024]{2,1,0:T(8,128)(2,1)S(1)}, u32[]{:S(2)}, u32[]{:S(2)}) async-start(bf16[4,32,1024]{2,1,0:T(8,128)(2,1)} %convert_element_type.138), calls=%async_computation | async-start | bytes 524288 | tf_op jit(solution)/shard_map/all_to_all | solution.py:160
  63.8 8.9 %all-to-all-done = bf16[4,32,1024]{2,1,0:T(8,128)(2,1)S(1)} async-done(((bf16[4,32,1024]{2,1,0:T(8,128)(2,1)}), bf16[4,32,1024]{2,1,0:T(8,128)(2,1)S(1)}, u32[]{:S(2)}, u32[]{:S(2)}) %all-to-all-start) | async-done | bytes 262176 | tf_op jit(solution)/shard_map/all_to_all | solution.py:160
  73.2 0.5 broadcast_in_dim.50
  73.9 0.3 convolution_convert_fusion
  74.2 22.0 %all_to_all.36 = bf16[4,24,4096]{2,1,0:T(8,128)(2,1)} all-to-all(bf16[4,24,4096]{2,1,0:T(8,128)(2,1)S(1)} %bitcast.106), channel_id=1, replica_groups=mesh['ctx'=8,'exp'=4] {'exp'}, dimensions={0} | all-to-all | bytes 1572864 | tf_op jit(solution)/shard_map/all_to_all | solution.py:169
  96.2 0.2 reduce-scatter.2.cloned.1.call-start
  96.5 43.6 %all-gather.7.cloned.1.call-done = bf16[768,4096]{1,0:T(8,128)(2,1)} async-done(((bf16[96,4096]{1,0:T(8,128)(2,1)}), bf16[768,4096]{1,0:T(8,128)(2,1)}) %all-gather.7.cloned.1.call-update) | async-done | bytes 6291472 | tf_op jit(solution)/shard_map/all_gather | solution.py:90
  140.1 30.9 %fusion.6 = bf16[768,4096]{1,0:T(8,128)(2,1)} fusion(bf16[1,1536,4096]{2,1,0:T(8,128)(2,1)} %param.27, bf16[768,4096]{1,0:T(8,128)(2,1)} %all-gather.7.cloned.1.call-done, bf16[1,4096,1536]{2,1,0:T(8,128)(2,1)} %param.26), kind=kOutput, calls=%fused_computation.10 | convolution fusion | flops 19336396800 | bytes 37748736 | tf_op jit(solution)/shard_map/dot_general | solution.py:96
  171.1 0.8 copy-done.2
  172.2 1.1 convolution_convert_fusion.1
  173.5 59.4 %reduce-scatter.2.cloned.1.call-done = bf16[96,4096]{1,0:T(8,128)(2,1)} async-done(((bf16[768,4096]{1,0:T(8,128)(2,1)}), bf16[96,4096]{1,0:T(8,128)(2,1)}) %reduce-scatter.2.cloned.1.call-update) | async-done | bytes 786448 | tf_op jit(solution)/shard_map/reduce_scatter | solution.py:95
  232.9 4.6 %all-to-all-start.2 = ((bf16[4,24,4096]{2,1,0:T(8,128)(2,1)}), bf16[4,24,4096]{2,1,0:T(8,128)(2,1)S(1)}, u32[]{:S(2)}, u32[]{:S(2)}) async-start(bf16[4,24,4096]{2,1,0:T(8,128)(2,1)} %bitcast.116), calls=%async_computation.3 | async-start | bytes 1572864 | tf_op jit(solution)/shard_map/all_to_all | solution.py:179
  237.5 25.8 %all-gather.11.cloned.1.call-done = bf16[128,64,128]{2,1,0:T(8,128)(2,1)} async-done(((bf16[16,64,128]{2,1,0:T(8,128)(2,1)}), bf16[128,64,128]{2,1,0:T(8,128)(2,1)}) %all-gather.11.cloned.1.call-update) | async-done | bytes 2097168 | tf_op jit(solution)/shard_map/all_gather | solution.py:21
  263.3 14.4 %while.31 = (s32[]{:T(128)}, f32[16,64,128]{2,1,0:T(8,128)S(1)}, s32[]{:T(128)}, bf16[8,16]{1,0:T(8,128)(2,1)}, bf16[8,16,64,128]{3,2,1,0:T(8,128)(2,1)}, /*index=5*/s32[]{:T(128)}, s32[]{:T(128)}, s32[]{:T(128)}, s32[]{:T(128)}) while((s32[]{:T(128)}, f32[16,64,128]{2,1,0:T(8,128)S(1)}, s32[]{:T(128)}, bf16[8,16]{1,0:T(8,128)(2,1)}, ...), condition=%wide.region_9.10_spmd.clone, body=%wide.region_8.9_spmd.clone.sunk | while | flops 655384 | bytes 1311047 | solution.py:35
  263.3 0.7 bitcast_convert_fusion.5
  264.0 1.1 fusion.67
  265.1 0.7 bitcast_convert_fusion.5
  265.8 1.1 fusion.67
  266.9 0.7 bitcast_convert_fusion.5
  267.6 1.1 fusion.67
  268.7 0.7 bitcast_convert_fusion.5
  269.4 1.1 fusion.67
  270.5 0.7 bitcast_convert_fusion.5
  271.2 1.1 fusion.67
  272.3 0.7 bitcast_convert_fusion.5
  273.0 1.1 fusion.67
  274.1 0.7 bitcast_convert_fusion.5
  274.8 1.1 fusion.67
  275.9 0.7 bitcast_convert_fusion.5
  276.6 1.1 fusion.67
  277.7 0.3 fusion.13
  278.0 0.7 copy.46
  278.7 4.6 %all-to-all-start.3 = ((bf16[32,4,1024]{2,0,1:T(8,128)(2,1)}), bf16[32,4,1024]{2,0,1:T(8,128)(2,1)S(1)}, u32[]{:S(2)}, u32[]{:S(2)}) async-start(bf16[32,4,1024]{2,0,1:T(8,128)(2,1)} %bitcast.95), calls=%async_computation.4 | async-start | bytes 524288 | tf_op jit(solution)/shard_map/all_to_all | solution.py:189
  283.3 0.4 fusion.19
  283.7 0.9 fusion.15
  284.6 1.0 copy.40
  285.6 7.0 %all-to-all-done.3 = bf16[32,4,1024]{2,0,1:T(8,128)(2,1)S(1)} async-done(((bf16[32,4,1024]{2,0,1:T(8,128)(2,1)}), bf16[32,4,1024]{2,0,1:T(8,128)(2,1)S(1)}, u32[]{:S(2)}, u32[]{:S(2)}) %all-to-all-start.3) | async-done | bytes 262176 | tf_op jit(solution)/shard_map/all_to_all | solution.py:189
  292.6 0.7 copy.61
  (82 shorter events, 2.5 us)
Async XLA Ops:
  7.2 26.7 %copy-start = (bf16[128,128]{1,0:T(8,128)(2,1)S(1)}, bf16[128,128]{1,0:T(8,128)(2,1)}, u32[]{:S(2)}) copy-start(bf16[128,128]{1,0:T(8,128)(2,1)} %param.19) | copy-start | bytes 98308
  7.2 48.9 %copy-start.18 = (f32[16]{0:T(128)S(1)}, f32[16]{0:T(128)}, u32[]{:S(2)}) copy-start(f32[16]{0:T(128)} %param.21) | copy-start | bytes 196
  7.2 39.4 %all-gather.9.cloned.1.call-start = ((), (), s32[]{:S(2)}) async-start(), calls=%async_computation.7 | async-start | bytes 2359296 | tf_op jit(solution)/shard_map/all_gather | solution.py:21
  8.0 5.5 %collective-permute-start = (bf16[3,1024]{1,0:T(4,128)(2,1)S(1)}, bf16[3,1024]{1,0:T(4,128)(2,1)S(1)}, u32[]{:S(2)}, u32[]{:S(2)}) collective-permute-start(bf16[3,1024]{1,0:T(4,128)(2,1)S(1)} %slice.29), channel_id=1, source_target_pairs={{0,4},{4,8},{8,12},{12,16},{16,20},{20,24},{24,28},{1,5},{5,9},{9,... | collective-permute-start | bytes 18440 | tf_op jit(solution)/shard_map/ppermute | solution.py:15
  12.2 45.1 %copy-start.3 = (f32[16,128]{1,0:T(8,128)}, f32[16,128]{1,0:T(8,128)S(1)}, u32[]{:S(2)}) copy-start(f32[16,128]{1,0:T(8,128)S(1)} %reduce_window_sum.23) | copy-start | bytes 24580
  12.4 3.5 %copy-start.5 = (f32[128,16]{0,1:T(8,128)}, f32[128,16]{0,1:T(8,128)S(1)}, u32[]{:S(2)}) copy-start(f32[128,16]{0,1:T(8,128)S(1)} %get-tuple-element.299) | copy-start | bytes 24580
  12.4 44.9 %copy-start.7 = (f32[128,16]{0,1:T(8,128)}, f32[128,16]{0,1:T(8,128)S(1)}, u32[]{:S(2)}) copy-start(f32[128,16]{0,1:T(8,128)S(1)} %get-tuple-element.298) | copy-start | bytes 24580
  33.8 29.8 %copy-start.12 = (pred[128,128]{1,0:T(8,128)(4,1)}, pred[128,128]{1,0:T(8,128)(4,1)S(1)}, u32[]{:S(2)}) copy-start(pred[128,128]{1,0:T(8,128)(4,1)S(1)} %iota_compare_fusion) | copy-start | bytes 49156
  34.8 38.1 %copy-start.9 = (f32[128,128]{1,0:T(8,128)}, f32[128,128]{1,0:T(8,128)S(1)}, u32[]{:S(2)}) copy-start(f32[128,128]{1,0:T(8,128)S(1)} %fusion.54) | copy-start | bytes 196612
  46.6 26.5 %copy-start.11 = (f32[4096]{0:T(1024)S(1)}, f32[4096]{0:T(1024)}, u32[]{:S(2)}) copy-start(f32[4096]{0:T(1024)} %param.23) | copy-start | bytes 49156
  55.6 17.4 %copy-start.16 = (bf16[8,16]{1,0:T(8,128)(2,1)}, bf16[8,16]{1,0:T(8,128)(2,1)S(1)}, u32[]{:S(2)}) copy-start(bf16[8,16]{1,0:T(8,128)(2,1)S(1)} %get-tuple-element.436) | copy-start | bytes 772
  58.8 13.9 %all-to-all-start = ((bf16[4,32,1024]{2,1,0:T(8,128)(2,1)}), bf16[4,32,1024]{2,1,0:T(8,128)(2,1)S(1)}, u32[]{:S(2)}, u32[]{:S(2)}) async-start(bf16[4,32,1024]{2,1,0:T(8,128)(2,1)} %convert_element_type.138), calls=%async_computation | async-start | bytes 524288 | tf_op jit(solution)/shard_map/all_to_all | solution.py:160
  63.4 76.6 %all-gather.7.cloned.1.call-start = ((), (), s32[]{:S(2)}) async-start(), calls=%async_computation.5 | async-start | bytes 7077888 | tf_op jit(solution)/shard_map/all_gather | solution.py:90
  63.8 107.2 %copy-start.14 = (s32[64]{0:T(128)}, s32[64]{0:T(128)S(1)}, u32[]{:S(2)}) copy-start(s32[64]{0:T(128)S(1)} %multiply_add_fusion) | copy-start | bytes 772
  96.2 136.7 %reduce-scatter.2.cloned.1.call-start = ((), (), s32[]{:S(2)}) async-start(), calls=%async_computation.6 | async-start | bytes 7077888 | tf_op jit(solution)/shard_map/reduce_scatter | solution.py:95
  171.0 1.0 copy-start.2
  171.0 1.2 copy-start.8
  171.0 2.4 copy-start.17
  171.0 2.3 copy-start.15
  171.0 112.3 %copy-start.1 = (bf16[128,128]{1,0:T(8,128)(2,1)S(1)}, bf16[128,128]{1,0:T(8,128)(2,1)}, u32[]{:S(2)}) copy-start(bf16[128,128]{1,0:T(8,128)(2,1)} %param.18) | copy-start | bytes 98308
  171.0 112.3 %copy-start.6 = (f32[128,16]{0,1:T(8,128)S(1)}, f32[128,16]{0,1:T(8,128)}, u32[]{:S(2)}) copy-start(f32[128,16]{0,1:T(8,128)} %copy-done.5) | copy-start | bytes 24580
  171.1 92.3 %all-gather.11.cloned.1.call-start = ((), (), s32[]{:S(2)}) async-start(), calls=%async_computation.8 | async-start | bytes 2359296 | tf_op jit(solution)/shard_map/all_gather | solution.py:21
  172.1 111.6 %copy-start.4 = (f32[16,128]{1,0:T(8,128)S(1)}, f32[16,128]{1,0:T(8,128)}, u32[]{:S(2)}) copy-start(f32[16,128]{1,0:T(8,128)} %copy-done.3) | copy-start | bytes 24580
  172.1 111.6 %copy-start.10 = (f32[128,128]{1,0:T(8,128)S(1)}, f32[128,128]{1,0:T(8,128)}, u32[]{:S(2)}) copy-start(f32[128,128]{1,0:T(8,128)} %copy-done.9) | copy-start | bytes 196612
  172.1 111.6 %copy-start.13 = (pred[128,128]{1,0:T(8,128)(4,1)S(1)}, pred[128,128]{1,0:T(8,128)(4,1)}, u32[]{:S(2)}) copy-start(pred[128,128]{1,0:T(8,128)(4,1)} %copy-done.12) | copy-start | bytes 49156
  172.1 111.6 %copy-start.19 = (f32[16]{0:T(128)S(1)}, f32[16]{0:T(128)}, u32[]{:S(2)}) copy-start(f32[16]{0:T(128)} %param.21) | copy-start | bytes 196
  232.9 44.8 %all-to-all-start.2 = ((bf16[4,24,4096]{2,1,0:T(8,128)(2,1)}), bf16[4,24,4096]{2,1,0:T(8,128)(2,1)S(1)}, u32[]{:S(2)}, u32[]{:S(2)}) async-start(bf16[4,24,4096]{2,1,0:T(8,128)(2,1)} %bitcast.116), calls=%async_computation.3 | async-start | bytes 1572864 | tf_op jit(solution)/shard_map/all_to_all | solution.py:179
  278.7 13.9 %all-to-all-start.3 = ((bf16[32,4,1024]{2,0,1:T(8,128)(2,1)}), bf16[32,4,1024]{2,0,1:T(8,128)(2,1)S(1)}, u32[]{:S(2)}, u32[]{:S(2)}) async-start(bf16[32,4,1024]{2,0,1:T(8,128)(2,1)} %bitcast.95), calls=%async_computation.4 | async-start | bytes 524288 | tf_op jit(solution)/shard_map/all_to_all | solution.py:189
Sparse Core Ops, SparseCore 0:
  16.0 30.4 all-gather.8
  96.4 43.6 all-gather.6
  171.1 61.7 reduce-scatter.1
  235.4 27.8 all-gather.10
where the time goes:
time: 301 us; the launch traced here: 300 us
  waiting for transfers between devices  157 us (52%)
  matrix products  38.4 us (13%)
  blocking collectives  36.5 us (12%)
  other arithmetic  26.4 us (9%)
  starting transfers between devices  16.4 us (5%)
  between operations  14.9 us (5%)
  local copies, waits for them, and re-layouts  10.3 us (3%)
    reduce_scatter x1, waiting for transfers between devices, expert_block(): lax.psum_scatter(jnp.dot(hidden, down_local, preferred_element_type=jnp.f...  59.4 us
    all_gather x1, waiting for transfers between devices, expert_block(): lax.all_gather(rows_in, 'ctx', axis=0, tiled=True)  43.6 us
    all_gather x2, waiting for transfers between devices, prefix(): lax.all_gather(part.astype(kind), axis)  37.6 us
    dot_general x1, matrix products, expert_block(): jnp.dot(hidden, down_local, preferred_element_type=jnp.float32)  30.9 us
    all_to_all x1, blocking collectives, shards(): lax.all_to_all(outgoing.reshape(experts, most_rows, normed.shape[1]), 'ex...  22 us
    select_n x16, other arithmetic, turn(): return jax.tree.map(lambda a, b: jnp.where(reached, a, b), new, before)  17.5 us
    unnamed x1, blocking collectives  14.5 us
    all_to_all x1, waiting for transfers between devices, shards(): lax.all_to_all(ssd_out, 'exp', split_axis=0, concat_axis=1, tiled=True)  8.94 us
  transfers between devices with their start and end apart: 8, of which 6 were waited for; matrix products, arithmetic and copies ran while one was open for 8% of the time, Pallas kernels for 0%

commit v1 on v0

--- a/solution.py
+++ b/solution.py
@@ -7,6 +7,15 @@
 TOPK = 2
 HIGHEST = lax.Precision.HIGHEST
 EPSILON = 1e-06
+lift_digits = lambda row_data: jnp.concatenate(
+    lax.all_to_all(
+        jnp.stack(jnp.split(row_data, lax.axis_size("exp"), 1), 0),
+        "exp",
+        split_axis=0,
+        concat_axis=0,
+    ),
+    axis=0,
+)
 
 
 def passed_along(block, axis, distance):
@@ -186,7 +195,7 @@
     combined = gather_back(
         dispatch, returned.reshape(experts * most_rows, normed.shape[1]), my_weights
     )
-    moe_out = lax.all_to_all(combined, "exp", split_axis=1, concat_axis=0, tiled=True)
+    moe_out = lift_digits(combined)
     return (moe_out, grad_conv)
 
 

time: 301 us -> 301 us (level)
  no operation moved by 1% of the time
where the time goes in v1:
time: 301 us; the launch traced here: 300 us
  waiting for transfers between devices  157 us (52%)
  matrix products  38.3 us (13%)
  blocking collectives  36.5 us (12%)
  other arithmetic  26.8 us (9%)
  starting transfers between devices  16.4 us (5%)
  between operations  14.9 us (5%)
  local copies, waits for them, and re-layouts  9.58 us (3%)
    reduce_scatter x1, waiting for transfers between devices, expert_block(): lax.psum_scatter(jnp.dot(hidden, down_local, preferred_element_type=jnp.f...  59.5 us
    all_gather x1, waiting for transfers between devices, expert_block(): lax.all_gather(rows_in, 'ctx', axis=0, tiled=True)  43.6 us
    all_gather x2, waiting for transfers between devices, prefix(): lax.all_gather(part.astype(kind), axis)  37.6 us
    dot_general x1, matrix products, expert_block(): jnp.dot(hidden, down_local, preferred_element_type=jnp.float32)  30.9 us
    all_to_all x1, blocking collectives, shards(): lax.all_to_all(outgoing.reshape(experts, most_rows, normed.shape[1]), 'ex...  22 us
    select_n x16, other arithmetic, turn(): return jax.tree.map(lambda a, b: jnp.where(reached, a, b), new, before)  17.5 us
    unnamed x1, blocking collectives  14.5 us
    all_to_all x1, waiting for transfers between devices, shards(): lax.all_to_all(ssd_out, 'exp', split_axis=0, concat_axis=1, tiled=True)  8.94 us
  transfers between devices with their start and end apart: 8, of which 6 were waited for; matrix products, arithmetic and copies ran while one was open for 8% of the time, Pallas kernels for 0%

profile of v1, /device:TPU:0, one launch (start us, length us, event | category | flops | bytes accessed | tf_op | source)
XLA Modules:
  0.0 299.6 jit_solution(188655138731517141)
XLA Ops:
  7.2 0.7 slice.29
  8.0 2.3 collective-permute-start
  10.3 0.9 fusion.53
  11.2 1.0 reduce_window_sum.23
  12.5 1.0 convert_element_type.128
  13.5 0.3 multiply_convert_fusion.2
  14.0 1.9 convolution_convert_fusion.2
  15.9 1.2 dynamic-slice
  18.0 0.2 dynamic-update-slice
  18.3 14.5 %all-reduce = bf16[128]{0:T(256)(128)(2,1)S(1)} all-reduce(bf16[128]{0:T(256)(128)(2,1)S(1)} %dynamic-update-slice), channel_id=2, replica_groups=mesh['ctx'=8,'exp'=4] {'ctx'}, use_global_device_ids=true, to_apply=%add | all-reduce | flops 128 | bytes 512
  32.8 0.8 constant_dynamic-slice_fusion
  33.8 0.9 fusion.54
  34.8 11.8 %all-gather.9.cloned.1.call-done = bf16[128,64,128]{2,1,0:T(8,128)(2,1)} async-done(((bf16[16,64,128]{2,1,0:T(8,128)(2,1)}), bf16[128,64,128]{2,1,0:T(8,128)(2,1)}) %all-gather.9.cloned.1.call-update) | async-done | bytes 2097168 | tf_op jit(solution)/shard_map/all_gather | solution.py:30
  46.6 9.1 %while.30 = (s32[]{:T(128)}, f32[16,64,128]{2,1,0:T(8,128)S(1)}, s32[]{:T(128)}, bf16[8,16]{1,0:T(8,128)(2,1)S(1)}, bf16[8,16,64,128]{3,2,1,0:T(8,128)(2,1)}, /*index=5*/s32[]{:T(128)}, s32[]{:T(128)}) while((s32[]{:T(128)}, f32[16,64,128]{2,1,0:T(8,128)S(1)}, s32[]{:T(128)}, bf16[8,16]{1,0:T(8,128)(2,1)S(1)}, ...), condition=%wide.region_4.5_spmd.clone, body=%wide.region_3.4_spmd.clone.sunk | while | flops 655380 | bytes 1310985 | solution.py:44
  46.6 1.1 fusion.66
  47.7 1.1 fusion.66
  48.8 1.1 fusion.66
  50.0 1.1 fusion.66
  51.1 1.1 fusion.66
  52.3 1.1 fusion.66
  53.4 1.1 fusion.66
  54.5 1.1 fusion.66
  55.6 0.4 fusion.18
  56.0 1.3 fusion.20
  57.4 0.4 copy.27
  57.8 1.1 convert_element_type.134
  58.8 4.6 %all-to-all-start = ((bf16[4,32,1024]{2,1,0:T(8,128)(2,1)}), bf16[4,32,1024]{2,1,0:T(8,128)(2,1)S(1)}, u32[]{:S(2)}, u32[]{:S(2)}) async-start(bf16[4,32,1024]{2,1,0:T(8,128)(2,1)} %convert_element_type.134), calls=%async_computation | async-start | bytes 524288 | tf_op jit(solution)/shard_map/all_to_all | solution.py:169
  63.8 8.9 %all-to-all-done = bf16[4,32,1024]{2,1,0:T(8,128)(2,1)S(1)} async-done(((bf16[4,32,1024]{2,1,0:T(8,128)(2,1)}), bf16[4,32,1024]{2,1,0:T(8,128)(2,1)S(1)}, u32[]{:S(2)}, u32[]{:S(2)}) %all-to-all-start) | async-done | bytes 262176 | tf_op jit(solution)/shard_map/all_to_all | solution.py:169
  73.2 0.5 broadcast_in_dim.50
  73.9 0.3 convolution_convert_fusion
  74.2 22.0 %all_to_all.25 = bf16[4,24,4096]{2,1,0:T(8,128)(2,1)} all-to-all(bf16[4,24,4096]{2,1,0:T(8,128)(2,1)S(1)} %bitcast.108), channel_id=1, replica_groups=mesh['ctx'=8,'exp'=4] {'exp'}, dimensions={0} | all-to-all | bytes 1572864 | tf_op jit(solution)/shard_map/all_to_all | solution.py:178
  96.2 0.2 reduce-scatter.2.cloned.1.call-start
  96.5 43.6 %all-gather.7.cloned.1.call-done = bf16[768,4096]{1,0:T(8,128)(2,1)} async-done(((bf16[96,4096]{1,0:T(8,128)(2,1)}), bf16[768,4096]{1,0:T(8,128)(2,1)}) %all-gather.7.cloned.1.call-update) | async-done | bytes 6291472 | tf_op jit(solution)/shard_map/all_gather | solution.py:99
  140.1 30.9 %fusion.6 = bf16[768,4096]{1,0:T(8,128)(2,1)} fusion(bf16[1,1536,4096]{2,1,0:T(8,128)(2,1)} %param.27, bf16[768,4096]{1,0:T(8,128)(2,1)} %all-gather.7.cloned.1.call-done, bf16[1,4096,1536]{2,1,0:T(8,128)(2,1)} %param.26), kind=kOutput, calls=%fused_computation.10 | convolution fusion | flops 19336396800 | bytes 37748736 | tf_op jit(solution)/shard_map/dot_general | solution.py:105
  171.1 0.8 copy-done.2
  172.1 1.1 convolution_convert_fusion.1
  173.5 59.5 %reduce-scatter.2.cloned.1.call-done = bf16[96,4096]{1,0:T(8,128)(2,1)} async-done(((bf16[768,4096]{1,0:T(8,128)(2,1)}), bf16[96,4096]{1,0:T(8,128)(2,1)}) %reduce-scatter.2.cloned.1.call-update) | async-done | bytes 786448 | tf_op jit(solution)/shard_map/reduce_scatter | solution.py:104
  232.9 4.6 %all-to-all-start.2 = ((bf16[4,24,4096]{2,1,0:T(8,128)(2,1)}), bf16[4,24,4096]{2,1,0:T(8,128)(2,1)S(1)}, u32[]{:S(2)}, u32[]{:S(2)}) async-start(bf16[4,24,4096]{2,1,0:T(8,128)(2,1)} %bitcast.117), calls=%async_computation.3 | async-start | bytes 1572864 | tf_op jit(solution)/shard_map/all_to_all | solution.py:188
  237.5 25.8 %all-gather.11.cloned.1.call-done = bf16[128,64,128]{2,1,0:T(8,128)(2,1)} async-done(((bf16[16,64,128]{2,1,0:T(8,128)(2,1)}), bf16[128,64,128]{2,1,0:T(8,128)(2,1)}) %all-gather.11.cloned.1.call-update) | async-done | bytes 2097168 | tf_op jit(solution)/shard_map/all_gather | solution.py:30
  263.3 14.1 %while.31 = (s32[]{:T(128)}, f32[16,64,128]{2,1,0:T(8,128)S(1)}, s32[]{:T(128)}, bf16[8,16]{1,0:T(8,128)(2,1)}, bf16[8,16,64,128]{3,2,1,0:T(8,128)(2,1)}, /*index=5*/s32[]{:T(128)}, s32[]{:T(128)}, s32[]{:T(128)}, s32[]{:T(128)}) while((s32[]{:T(128)}, f32[16,64,128]{2,1,0:T(8,128)S(1)}, s32[]{:T(128)}, bf16[8,16]{1,0:T(8,128)(2,1)}, ...), condition=%wide.region_9.10_spmd.clone, body=%wide.region_8.9_spmd.clone.sunk | while | flops 655384 | bytes 1311047 | solution.py:44
  263.3 0.6 bitcast_convert_fusion.5
  264.0 1.1 fusion.67
  265.1 0.6 bitcast_convert_fusion.5
  265.7 1.1 fusion.67
  266.8 0.6 bitcast_convert_fusion.5
  267.5 1.1 fusion.67
  268.6 0.6 bitcast_convert_fusion.5
  269.2 1.1 fusion.67
  270.4 0.6 bitcast_convert_fusion.5
  271.0 1.1 fusion.67
  272.1 0.6 bitcast_convert_fusion.5
  272.8 1.1 fusion.67
  273.9 0.6 bitcast_convert_fusion.5
  274.5 1.1 fusion.67
  275.6 0.6 bitcast_convert_fusion.5
  276.3 1.1 fusion.67
  277.4 0.3 fusion.13
  277.7 0.7 pad_maximum_fusion.1
  278.5 4.6 %all-to-all-start.3 = ((bf16[4,32,1024]{2,1,0:T(8,128)(2,1)}), bf16[4,32,1024]{2,1,0:T(8,128)(2,1)S(1)}, u32[]{:S(2)}, u32[]{:S(2)}) async-start(bf16[4,32,1024]{2,1,0:T(8,128)(2,1)} %pad_maximum_fusion.1), calls=%async_computation.4 | async-start | bytes 524288 | tf_op jit(solution)/shard_map/all_to_all | solution.py:11
  283.1 0.4 fusion.19
  283.5 0.9 fusion.15
  284.4 1.0 copy.31
  285.4 7.0 %all-to-all-done.3 = bf16[4,32,1024]{2,1,0:T(8,128)(2,1)S(1)} async-done(((bf16[4,32,1024]{2,1,0:T(8,128)(2,1)}), bf16[4,32,1024]{2,1,0:T(8,128)(2,1)S(1)}, u32[]{:S(2)}, u32[]{:S(2)}) %all-to-all-start.3) | async-done | bytes 262176 | tf_op jit(solution)/shard_map/all_to_all | solution.py:11
  292.4 0.7 copy.49
  (83 shorter events, 2.5 us)
Async XLA Ops:
  7.2 26.7 %copy-start = (bf16[128,128]{1,0:T(8,128)(2,1)S(1)}, bf16[128,128]{1,0:T(8,128)(2,1)}, u32[]{:S(2)}) copy-start(bf16[128,128]{1,0:T(8,128)(2,1)} %param.19) | copy-start | bytes 98308
  7.2 48.9 %copy-start.18 = (f32[16]{0:T(128)S(1)}, f32[16]{0:T(128)}, u32[]{:S(2)}) copy-start(f32[16]{0:T(128)} %param.21) | copy-start | bytes 196
  7.2 39.4 %all-gather.9.cloned.1.call-start = ((), (), s32[]{:S(2)}) async-start(), calls=%async_computation.7 | async-start | bytes 2359296 | tf_op jit(solution)/shard_map/all_gather | solution.py:30
  8.0 5.5 %collective-permute-start = (bf16[3,1024]{1,0:T(4,128)(2,1)S(1)}, bf16[3,1024]{1,0:T(4,128)(2,1)S(1)}, u32[]{:S(2)}, u32[]{:S(2)}) collective-permute-start(bf16[3,1024]{1,0:T(4,128)(2,1)S(1)} %slice.29), channel_id=1, source_target_pairs={{0,4},{4,8},{8,12},{12,16},{16,20},{20,24},{24,28},{1,5},{5,9},{9,... | collective-permute-start | bytes 18440 | tf_op jit(solution)/shard_map/ppermute | solution.py:24
  12.2 45.1 %copy-start.3 = (f32[16,128]{1,0:T(8,128)}, f32[16,128]{1,0:T(8,128)S(1)}, u32[]{:S(2)}) copy-start(f32[16,128]{1,0:T(8,128)S(1)} %reduce_window_sum.23) | copy-start | bytes 24580
  12.4 3.5 %copy-start.5 = (f32[128,16]{0,1:T(8,128)}, f32[128,16]{0,1:T(8,128)S(1)}, u32[]{:S(2)}) copy-start(f32[128,16]{0,1:T(8,128)S(1)} %get-tuple-element.301) | copy-start | bytes 24580
  12.4 44.9 %copy-start.7 = (f32[128,16]{0,1:T(8,128)}, f32[128,16]{0,1:T(8,128)S(1)}, u32[]{:S(2)}) copy-start(f32[128,16]{0,1:T(8,128)S(1)} %get-tuple-element.300) | copy-start | bytes 24580
  33.8 29.8 %copy-start.12 = (pred[128,128]{1,0:T(8,128)(4,1)}, pred[128,128]{1,0:T(8,128)(4,1)S(1)}, u32[]{:S(2)}) copy-start(pred[128,128]{1,0:T(8,128)(4,1)S(1)} %iota_compare_fusion) | copy-start | bytes 49156
  34.8 38.1 %copy-start.9 = (f32[128,128]{1,0:T(8,128)}, f32[128,128]{1,0:T(8,128)S(1)}, u32[]{:S(2)}) copy-start(f32[128,128]{1,0:T(8,128)S(1)} %fusion.54) | copy-start | bytes 196612
  46.6 26.5 %copy-start.11 = (f32[4096]{0:T(1024)S(1)}, f32[4096]{0:T(1024)}, u32[]{:S(2)}) copy-start(f32[4096]{0:T(1024)} %param.23) | copy-start | bytes 49156
  55.6 17.4 %copy-start.16 = (bf16[8,16]{1,0:T(8,128)(2,1)}, bf16[8,16]{1,0:T(8,128)(2,1)S(1)}, u32[]{:S(2)}) copy-start(bf16[8,16]{1,0:T(8,128)(2,1)S(1)} %get-tuple-element.438) | copy-start | bytes 772
  58.8 13.9 %all-to-all-start = ((bf16[4,32,1024]{2,1,0:T(8,128)(2,1)}), bf16[4,32,1024]{2,1,0:T(8,128)(2,1)S(1)}, u32[]{:S(2)}, u32[]{:S(2)}) async-start(bf16[4,32,1024]{2,1,0:T(8,128)(2,1)} %convert_element_type.134), calls=%async_computation | async-start | bytes 524288 | tf_op jit(solution)/shard_map/all_to_all | solution.py:169
  63.4 76.6 %all-gather.7.cloned.1.call-start = ((), (), s32[]{:S(2)}) async-start(), calls=%async_computation.5 | async-start | bytes 7077888 | tf_op jit(solution)/shard_map/all_gather | solution.py:99
  63.8 107.2 %copy-start.14 = (s32[64]{0:T(128)}, s32[64]{0:T(128)S(1)}, u32[]{:S(2)}) copy-start(s32[64]{0:T(128)S(1)} %multiply_add_fusion) | copy-start | bytes 772
  96.2 136.7 %reduce-scatter.2.cloned.1.call-start = ((), (), s32[]{:S(2)}) async-start(), calls=%async_computation.6 | async-start | bytes 7077888 | tf_op jit(solution)/shard_map/reduce_scatter | solution.py:104
  171.0 1.0 copy-start.2
  171.0 1.1 copy-start.8
  171.0 2.4 copy-start.17
  171.0 2.3 copy-start.15
  171.0 112.0 %copy-start.1 = (bf16[128,128]{1,0:T(8,128)(2,1)S(1)}, bf16[128,128]{1,0:T(8,128)(2,1)}, u32[]{:S(2)}) copy-start(bf16[128,128]{1,0:T(8,128)(2,1)} %param.18) | copy-start | bytes 98308
  171.0 112.0 %copy-start.6 = (f32[128,16]{0,1:T(8,128)S(1)}, f32[128,16]{0,1:T(8,128)}, u32[]{:S(2)}) copy-start(f32[128,16]{0,1:T(8,128)} %copy-done.5) | copy-start | bytes 24580
  171.1 92.3 %all-gather.11.cloned.1.call-start = ((), (), s32[]{:S(2)}) async-start(), calls=%async_computation.8 | async-start | bytes 2359296 | tf_op jit(solution)/shard_map/all_gather | solution.py:30
  173.2 110.2 %copy-start.4 = (f32[16,128]{1,0:T(8,128)S(1)}, f32[16,128]{1,0:T(8,128)}, u32[]{:S(2)}) copy-start(f32[16,128]{1,0:T(8,128)} %copy-done.3) | copy-start | bytes 24580
  173.2 110.3 %copy-start.10 = (f32[128,128]{1,0:T(8,128)S(1)}, f32[128,128]{1,0:T(8,128)}, u32[]{:S(2)}) copy-start(f32[128,128]{1,0:T(8,128)} %copy-done.9) | copy-start | bytes 196612
  173.2 110.3 %copy-start.13 = (pred[128,128]{1,0:T(8,128)(4,1)S(1)}, pred[128,128]{1,0:T(8,128)(4,1)}, u32[]{:S(2)}) copy-start(pred[128,128]{1,0:T(8,128)(4,1)} %copy-done.12) | copy-start | bytes 49156
  173.2 110.3 %copy-start.19 = (f32[16]{0:T(128)S(1)}, f32[16]{0:T(128)}, u32[]{:S(2)}) copy-start(f32[16]{0:T(128)} %param.21) | copy-start | bytes 196
  232.9 44.5 %all-to-all-start.2 = ((bf16[4,24,4096]{2,1,0:T(8,128)(2,1)}), bf16[4,24,4096]{2,1,0:T(8,128)(2,1)S(1)}, u32[]{:S(2)}, u32[]{:S(2)}) async-start(bf16[4,24,4096]{2,1,0:T(8,128)(2,1)} %bitcast.117), calls=%async_computation.3 | async-start | bytes 1572864 | tf_op jit(solution)/shard_map/all_to_all | solution.py:188
  278.5 13.9 %all-to-all-start.3 = ((bf16[4,32,1024]{2,1,0:T(8,128)(2,1)}), bf16[4,32,1024]{2,1,0:T(8,128)(2,1)S(1)}, u32[]{:S(2)}, u32[]{:S(2)}) async-start(bf16[4,32,1024]{2,1,0:T(8,128)(2,1)} %pad_maximum_fusion.1), calls=%async_computation.4 | async-start | bytes 524288 | tf_op jit(solution)/shard_map/all_to_all | solution.py:11
Sparse Core Ops, SparseCore 0:
  16.0 30.4 all-gather.8
  96.4 43.6 all-gather.6
  171.1 61.7 reduce-scatter.1
  235.4 27.8 all-gather.10
